TPU v7x, 32 devices: a whole 2x2x4 slice. The times are simulated.
32 devices in a mesh: dp: 16 (over z, x, core), tensor: 2 (over y).
Axes of the slice: x: 2, y: 2, z: 4, core: 2. Of those that a mesh axis runs over, the one named last changes fastest.
Arguments:
- layer_input: bfloat16 [16384, 1024], P('dp'), may hold values from -6 to 6
- segments: int32 [16, 1024], P('dp'), may hold values from 0 to 3, never falling along the last dimension, each value on 1 to 512 neighbouring positions
- expert_choice: int32 [16384, 2], P('dp'), may hold values from 0 to 3, as said below
- dispatch_order: int32 [16, 2048], P('dp'), may hold values from 0 to 2047, each once within a row
- norm_gain_one: float32 [1024], replicated, may hold values from 0.5 to 1.5
- w_query: bfloat16 [1024, 1024], P(None, 'tensor'), may hold values from -0.1875 to 0.1875
- w_key: bfloat16 [1024, 512], P(None, 'tensor'), may hold values from -0.1875 to 0.1875
- w_value: bfloat16 [1024, 512], P(None, 'tensor'), may hold values from -0.1875 to 0.1875
- w_out: bfloat16 [1024, 1024], P('tensor'), may hold values from -1 to 1
- norm_gain_two: float32 [1024], replicated, may hold values from 0.5 to 1.5
- w_router: bfloat16 [1024, 4], replicated, may hold values from -0.125 to 0.125
- w_gate: bfloat16 [4, 1024, 512], P(None, None, 'tensor'), may hold values from -0.1875 to 0.1875
- w_up: bfloat16 [4, 1024, 512], P(None, None, 'tensor'), may hold values from -0.1875 to 0.1875
- w_down: bfloat16 [4, 512, 1024], P(None, 'tensor'), may hold values from -0.5 to 0.5
- out_grad: bfloat16 [16384, 1024], P('dp'), may hold values from -6 to 6
Outputs:
- layer_output: bfloat16 [16384, 1024], P('dp')
- input_grad: float32 [16384, 1024], P('dp')
- norm_gain_one_grad: float32 [1024], replicated
- w_query_grad: float32 [1024, 1024], P(None, 'tensor')
- w_key_grad: float32 [1024, 512], P(None, 'tensor')
- w_value_grad: float32 [1024, 512], P(None, 'tensor')
- w_out_grad: float32 [1024, 1024], P('tensor')
- norm_gain_two_grad: float32 [1024], replicated
- w_router_grad: float32 [1024, 4], replicated
- w_gate_grad: float32 [4, 1024, 512], P(None, None, 'tensor')
- w_up_grad: float32 [4, 1024, 512], P(None, None, 'tensor')
- w_down_grad: float32 [4, 512, 1024], P(None, 'tensor')
Inputs may be any that keep to these rules, and one draw needn't show every extreme that they name: `segments`: along each sequence the segment numbers never fall; a document has at most 512 tokens. `expert_choice`: each token names 2 different experts. In each sequence one expert is named by exactly 832 of its tokens, and each other expert by fewer. `dispatch_order`: each row is a permutation of the pair numbers t * 2 + k of one sequence.
All inputs are finite; a program needn't handle non-finite values.
Results may differ from a plain program's by a relative error of at most 0.014.
The roundings to bfloat16 on the way count: a program that leaves them out, or rounds other values in their place, can miss the bound.
Values sent between devices are 32-bit elements; how exact they have to be, the bound alone decides.
No kernel may reach another device: no remote copies, remote signals or barrier semaphores. Data moves between devices by JAX's collectives and lax.ppermute only.
A program may use at most 1.0625 GiB of HBM per device.

v0:
```python
import jax
import jax.numpy as jnp
from jax import lax
from jax.sharding import PartitionSpec as P

D = 1024
HEAD_DIM = 64
EXPERTS = 4
TOPK = 2
CAP = 640


norm_eps = 1e-05
masked_value = -1e30


def normalize(values):
    inverse = lax.rsqrt(jnp.mean(values * values, axis=-1, keepdims=True) + norm_eps)
    return (values * inverse, inverse)


def norm_back(grad_normed, normed, inverse, gain_vec):
    scaled = grad_normed * gain_vec
    mean_term = jnp.mean(scaled * normed, axis=-1, keepdims=True)
    return (inverse * (scaled - normed * mean_term), jnp.sum(grad_normed * normed, axis=0))


def softmax_last(values):
    peak_value = jnp.max(values, axis=-1, keepdims=True)
    raised = jnp.exp(values - peak_value)
    return raised / jnp.sum(raised, axis=-1, keepdims=True)


def dispatch_tables(choice_rows, order_row):
    pair_count = order_row.shape[0]
    pair_expert = choice_rows.reshape(-1)
    ordered = pair_expert[order_row]
    expert_ids = jnp.arange(EXPERTS, dtype=jnp.int32)
    one_hot = (ordered[:, None] == expert_ids[None, :]).astype(jnp.int32)
    earlier = jnp.sum((jnp.cumsum(one_hot, axis=0) - one_hot) * one_hot, axis=1)
    target = jnp.where(earlier < CAP, ordered * CAP + earlier, EXPERTS * CAP)
    pair_target = jnp.zeros((pair_count,), jnp.int32).at[order_row].set(target)
    pair_ids = jnp.arange(pair_count, dtype=jnp.int32)
    empty_token = choice_rows.shape[0]
    slot_token = (
        jnp.full((EXPERTS * CAP + 1,), empty_token, jnp.int32).at[pair_target].set(pair_ids // TOPK)
    )
    slot_pair = jnp.full((EXPERTS * CAP + 1,), pair_count, jnp.int32).at[pair_target].set(pair_ids)
    return (slot_token[: EXPERTS * CAP], slot_pair[: EXPERTS * CAP])


def block_scores(query_block, key_heads, seg_query, seg_keys, begin_row, score_scale):
    scores = (
        jnp.einsum("rkgd,ckd->kgrc", query_block, key_heads, preferred_element_type=jnp.float32)
        * score_scale
    )
    row_pos = begin_row + jnp.arange(query_block.shape[0], dtype=jnp.int32)
    col_pos = jnp.arange(key_heads.shape[0], dtype=jnp.int32)
    allowed = (seg_query[:, None] == seg_keys[None, :]) & (col_pos[None, :] <= row_pos[:, None])
    return jnp.where(allowed, scores, masked_value)


def pack_rows(arrays, parts_count):
    flattened = jnp.concatenate([member.reshape(-1) for member in arrays])
    padding = -flattened.shape[0] % parts_count
    return flattened.reshape(parts_count, -1)


def unpack_rows(packed, arrays):
    flattened = packed.reshape(-1)
    result = []
    offset = 0
    for member in arrays:
        result.append(flattened[offset : offset + member.size].reshape(member.shape))
        offset = offset + member.size
    return result


def per_device(
    layer_input,
    segments,
    expert_choice,
    dispatch_order,
    norm_gain_one,
    w_query,
    w_key,
    w_value,
    w_out,
    norm_gain_two,
    w_router,
    w_gate,
    w_up,
    w_down,
    out_grad,
):
    length = layer_input.shape[0]
    score_scale = HEAD_DIM ** (-0.5)
    local_heads = w_query.shape[1] // HEAD_DIM
    local_kv = w_key.shape[1] // HEAD_DIM
    group_size = local_heads // local_kv
    block_rows = min(512, length)
    parts_count = lax.axis_size("dp")
    seg_ids = segments[0]
    residual = layer_input.astype(jnp.float32)
    normed_one, inverse_one = normalize(residual)
    input_one = (normed_one * norm_gain_one).astype(jnp.bfloat16)
    query_heads = (
        jnp.dot(input_one, w_query, preferred_element_type=jnp.float32)
        .astype(jnp.bfloat16)
        .reshape(length, local_kv, group_size, HEAD_DIM)
    )
    key_heads = (
        jnp.dot(input_one, w_key, preferred_element_type=jnp.float32)
        .astype(jnp.bfloat16)
        .reshape(length, local_kv, HEAD_DIM)
    )
    value_heads = (
        jnp.dot(input_one, w_value, preferred_element_type=jnp.float32)
        .astype(jnp.bfloat16)
        .reshape(length, local_kv, HEAD_DIM)
    )
    heads_out = []
    log_sums = []
    for begin_row in range(0, length, block_rows):
        finish = begin_row + block_rows
        scores = block_scores(
            query_heads[begin_row:finish],
            key_heads[:finish],
            seg_ids[begin_row:finish],
            seg_ids[:finish],
            begin_row,
            score_scale,
        )
        row_peak = jnp.max(scores, axis=-1, keepdims=True)
        raised = jnp.exp(scores - row_peak)
        row_total = jnp.sum(raised, axis=-1, keepdims=True)
        probs_low = (raised / row_total).astype(jnp.bfloat16)
        heads_out.append(
            jnp.einsum(
                "kgrc,ckd->rkgd",
                probs_low,
                value_heads[:finish],
                preferred_element_type=jnp.float32,
            ).astype(jnp.bfloat16)
        )
        log_sums.append(row_peak + jnp.log(row_total))
    attended = jnp.concatenate(heads_out, axis=0).reshape(length, local_heads * HEAD_DIM)
    attn_part = jnp.dot(attended, w_out, preferred_element_type=jnp.float32)
    attn_total = lax.psum(attn_part, "tensor")
    middle = residual + attn_total
    normed_two, inverse_two = normalize(middle)
    input_two = (normed_two * norm_gain_two).astype(jnp.bfloat16)
    logits = jnp.dot(input_two, w_router, preferred_element_type=jnp.float32)
    choice_hot = (
        expert_choice[:, :, None] == jnp.arange(EXPERTS, dtype=jnp.int32)[None, None, :]
    ).astype(jnp.float32)
    picked = jnp.sum(logits[:, None, :] * choice_hot, axis=-1)
    gating = softmax_last(picked)
    slot_token, slot_pair = dispatch_tables(expert_choice, dispatch_order[0])
    padded = jnp.concatenate([input_two, jnp.zeros((1, D), jnp.bfloat16)], axis=0)
    routed_rows = padded[slot_token].reshape(EXPERTS, CAP, D)
    pair_total = length * TOPK
    gate_flat = jnp.concatenate([gating.reshape(-1), jnp.zeros((1,), jnp.float32)])
    slot_weight = gate_flat[slot_pair]
    gate_proj = jnp.einsum("ecd,edf->ecf", routed_rows, w_gate, preferred_element_type=jnp.float32)
    up_proj = jnp.einsum("ecd,edf->ecf", routed_rows, w_up, preferred_element_type=jnp.float32)
    sigma_gate = jax.nn.sigmoid(gate_proj)
    activated = gate_proj * sigma_gate
    hidden = (activated * up_proj).astype(jnp.bfloat16)
    expert_part = jnp.einsum(
        "ecf,efd->ecd", hidden, w_down, preferred_element_type=jnp.float32
    ).reshape(EXPERTS * CAP, D)
    routed_part = (
        jnp.zeros((length + 1, D), jnp.float32)
        .at[slot_token]
        .add(slot_weight[:, None] * expert_part)[:length]
    )
    routed_total = lax.psum(routed_part, "tensor")
    block_out = (middle + routed_total).astype(jnp.bfloat16)
    grad_top = out_grad.astype(jnp.float32)
    grad_padded = jnp.concatenate([grad_top, jnp.zeros((1, D), jnp.float32)], axis=0)
    slot_grad = grad_padded[slot_token]
    grad_expert = (slot_weight[:, None] * slot_grad).astype(jnp.bfloat16).reshape(EXPERTS, CAP, D)
    gate_slot_part = jnp.sum(slot_grad * expert_part, axis=-1)
    gate_pair_part = (
        jnp.zeros((pair_total + 1,), jnp.float32)
        .at[slot_pair]
        .add(gate_slot_part)[:pair_total]
        .reshape(length, TOPK)
    )
    grad_hidden = jnp.einsum(
        "ecd,efd->ecf", grad_expert, w_down, preferred_element_type=jnp.float32
    )
    grad_wdown = jnp.einsum("ecf,ecd->efd", hidden, grad_expert, preferred_element_type=jnp.float32)
    grad_gate_proj = (
        grad_hidden * up_proj * sigma_gate * (1.0 + gate_proj * (1.0 - sigma_gate))
    ).astype(jnp.bfloat16)
    grad_up_proj = (grad_hidden * activated).astype(jnp.bfloat16)
    grad_wgate = jnp.einsum(
        "ecd,ecf->edf", routed_rows, grad_gate_proj, preferred_element_type=jnp.float32
    )
    grad_wup = jnp.einsum(
        "ecd,ecf->edf", routed_rows, grad_up_proj, preferred_element_type=jnp.float32
    )
    grad_rows = jnp.einsum(
        "ecf,edf->ecd", grad_gate_proj, w_gate, preferred_element_type=jnp.float32
    )
    grad_rows = (
        grad_rows
        + jnp.einsum("ecf,edf->ecd", grad_up_proj, w_up, preferred_element_type=jnp.float32)
    ).reshape(EXPERTS * CAP, D)
    routed_grad_part = (
        jnp.zeros((length + 1, D), jnp.float32).at[slot_token].add(grad_rows)[:length]
    )
    routed_grad, gate_pair_grad = lax.psum((routed_grad_part, gate_pair_part), "tensor")
    grad_picked = gating * (
        gate_pair_grad - jnp.sum(gating * gate_pair_grad, axis=-1, keepdims=True)
    )
    grad_logits = jnp.sum(grad_picked[:, :, None] * choice_hot, axis=1).astype(jnp.bfloat16)
    grad_router = jnp.einsum(
        "td,te->de", input_two, grad_logits, preferred_element_type=jnp.float32
    )
    grad_input_two = routed_grad + jnp.einsum(
        "te,de->td", grad_logits, w_router, preferred_element_type=jnp.float32
    )
    grad_middle_norm, grad_gain_two = norm_back(
        grad_input_two, normed_two, inverse_two, norm_gain_two
    )
    grad_middle = grad_top + grad_middle_norm
    expert_bucket = [grad_wgate, grad_wup, grad_wdown, grad_router, grad_gain_two]
    grad_attn = grad_middle.astype(jnp.bfloat16)
    grad_wout = jnp.einsum("tn,td->nd", attended, grad_attn, preferred_element_type=jnp.float32)
    grad_heads = (
        jnp.einsum("td,nd->tn", grad_attn, w_out, preferred_element_type=jnp.float32)
        .astype(jnp.bfloat16)
        .reshape(length, local_kv, group_size, HEAD_DIM)
    )
    grad_keys_sum = jnp.zeros((length, local_kv, HEAD_DIM), jnp.float32)
    grad_values_sum = jnp.zeros((length, local_kv, HEAD_DIM), jnp.float32)
    grad_query_list = []
    for index_block, begin_row in enumerate(range(0, length, block_rows)):
        finish = begin_row + block_rows
        query_block = query_heads[begin_row:finish]
        scores = block_scores(
            query_block,
            key_heads[:finish],
            seg_ids[begin_row:finish],
            seg_ids[:finish],
            begin_row,
            score_scale,
        )
        probs_exact = jnp.exp(scores - log_sums[index_block])
        probs_low = probs_exact.astype(jnp.bfloat16)
        grad_out_block = grad_heads[begin_row:finish]
        grad_probs = jnp.einsum(
            "rkgd,ckd->kgrc",
            grad_out_block,
            value_heads[:finish],
            preferred_element_type=jnp.float32,
        )
        row_dot = jnp.sum(probs_exact * grad_probs, axis=-1, keepdims=True)
        grad_scores = (probs_exact * (grad_probs - row_dot)).astype(jnp.bfloat16)
        grad_query_list.append(
            (
                jnp.einsum(
                    "kgrc,ckd->rkgd",
                    grad_scores,
                    key_heads[:finish],
                    preferred_element_type=jnp.float32,
                )
                * score_scale
            ).astype(jnp.bfloat16)
        )
        grad_keys_sum = grad_keys_sum.at[:finish].add(
            jnp.einsum(
                "kgrc,rkgd->ckd", grad_scores, query_block, preferred_element_type=jnp.float32
            )
            * score_scale
        )
        grad_values_sum = grad_values_sum.at[:finish].add(
            jnp.einsum(
                "kgrc,rkgd->ckd", probs_low, grad_out_block, preferred_element_type=jnp.float32
            )
        )
    grad_query = jnp.concatenate(grad_query_list, axis=0).reshape(length, local_heads * HEAD_DIM)
    grad_keys = grad_keys_sum.astype(jnp.bfloat16).reshape(length, local_kv * HEAD_DIM)
    grad_values = grad_values_sum.astype(jnp.bfloat16).reshape(length, local_kv * HEAD_DIM)
    grad_wquery = jnp.einsum("td,tn->dn", input_one, grad_query, preferred_element_type=jnp.float32)
    grad_wkey = jnp.einsum("td,tn->dn", input_one, grad_keys, preferred_element_type=jnp.float32)
    grad_wvalue = jnp.einsum(
        "td,tn->dn", input_one, grad_values, preferred_element_type=jnp.float32
    )
    input_grad_part = jnp.einsum(
        "tn,dn->td", grad_query, w_query, preferred_element_type=jnp.float32
    )
    input_grad_part = input_grad_part + jnp.einsum(
        "tn,dn->td", grad_keys, w_key, preferred_element_type=jnp.float32
    )
    input_grad_part = input_grad_part + jnp.einsum(
        "tn,dn->td", grad_values, w_value, preferred_element_type=jnp.float32
    )
    input_grad_one = lax.psum(input_grad_part, "tensor")
    grad_resid_norm, grad_gain_one = norm_back(
        input_grad_one, normed_one, inverse_one, norm_gain_one
    )
    grad_input = grad_middle + grad_resid_norm
    attention_bucket = [grad_gain_one, grad_wquery, grad_wkey, grad_wvalue, grad_wout]
    joined = expert_bucket + attention_bucket
    joined_shares = lax.psum_scatter(
        pack_rows(joined, parts_count), "dp", scatter_dimension=0, tiled=True
    )
    summed = unpack_rows(lax.all_gather(joined_shares, "dp", axis=0, tiled=True), joined)
    return (
        block_out,
        grad_input,
        summed[5],
        summed[6],
        summed[7],
        summed[8],
        summed[9],
        summed[4],
        summed[3],
        summed[0],
        summed[1],
        summed[2],
    )


def solution(mesh):
    in_specs = (
        P("dp", None),
        P("dp", None),
        P("dp", None),
        P("dp", None),
        P(),
        P(None, "tensor"),
        P(None, "tensor"),
        P(None, "tensor"),
        P("tensor", None),
        P(),
        P(),
        P(None, None, "tensor"),
        P(None, None, "tensor"),
        P(None, "tensor", None),
        P("dp", None),
    )
    out_specs = (
        P("dp", None),
        P("dp", None),
        P(),
        P(None, "tensor"),
        P(None, "tensor"),
        P(None, "tensor"),
        P("tensor", None),
        P(),
        P(),
        P(None, None, "tensor"),
        P(None, None, "tensor"),
        P(None, "tensor", None),
    )
    return jax.shard_map(
        per_device, mesh=mesh, in_specs=in_specs, out_specs=out_specs, check_vma=False
    )
```

profile of v0, /device:TPU:0, one launch (start us, length us, event | category | flops | bytes accessed | tf_op | source)
XLA Modules:
  0.0 2475.2 jit_solution(9334685906188009340)
XLA Ops:
  22.9 7.6 fusion.99
  30.5 8.0 fusion.3
  38.5 7.5 fusion.61
  51.2 11.8 gather_fusion
  64.7 8.0 scatter_custom_fusion
  72.7 8.1 scatter_custom_fusion.1
  80.8 8.1 scatter_custom_fusion.2
  93.0 14.6 gather_fusion.3
  108.3 52.9 %all-reduce.11.cloned.1.call-done = f32[1024,1024]{1,0:T(8,128)} async-done(((f32[1024,1024]{1,0:T(8,128)}), f32[1024,1024]{1,0:T(8,128)}) %all-reduce.11.cloned.1.call-update) | async-done | bytes 4194320 | tf_op jit(solution)/shard_map/psum | solution.py:149
  170.7 14.0 gather_fusion.2
  184.6 4.8 fusion.103
  189.5 6.0 multiply_convert_fusion.4
  195.5 5.6 multiply_reduce_fusion
  201.1 15.2 scatter_custom_fusion.5
  217.0 5.0 psum.38
  222.6 13.8 gather_fusion.1
  236.4 9.7 multiply_convert_fusion.2
  259.9 4.6 copy.110
  264.5 5.7 convolution_add_fusion
  270.2 25.6 %scatter_custom_fusion.4 = f32[1025,1024]{1,0:T(8,128)} fusion(s32[2560]{0:T(1024)S(1)} %compare_select_fusion.2, f32[2560,1024]{1,0:T(8,128)} %bitcast.241, f32[]{:T(128)} %constant.162.clone.1), kind=kCustom, calls=%fused_computation.69 | custom fusion | flops 2621440 | bytes 4198912 | tf_op jit(solution)/shard_map/scatter-add | solution.py:213
  295.7 4.8 slice.248
  300.6 4.6 constant_dynamic-update-slice_fusion.9
  307.5 8.6 bitcast_multiply_fusion.1
  316.1 25.5 %scatter_custom_fusion.3 = f32[1025,1024]{1,0:T(8,128)} fusion(s32[2560]{0:T(1024)S(1)} %compare_select_fusion.2, f32[2560,1024]{1,0:T(8,128)} %bitcast_multiply_fusion.1, f32[]{:T(128)} %constant.162.clone.1), kind=kCustom, calls=%fused_computation.71 | custom fusion | flops 2621440 | bytes 4198912 | tf_op jit(solution)/shard_map/scatter-add | solution.py:176
  341.6 5.0 slice.247
  346.6 6.0 fusion.35
  355.6 53.0 %all-reduce.13.cloned.1.call-done = f32[1024,1024]{1,0:T(8,128)} async-done(((f32[1024,1024]{1,0:T(8,128)}), f32[1024,1024]{1,0:T(8,128)}) %all-reduce.13.cloned.1.call-update) | async-done | bytes 4194320 | tf_op jit(solution)/shard_map/psum | solution.py:215
  408.6 5.8 multiply_reduce_fusion.1
  419.5 5.0 fusion.7
  424.6 4.8 fusion.9
  433.5 8.2 fusion
  447.3 8.7 fusion.2
  467.0 4.6 constant_dynamic-update-slice_fusion.7
  489.0 176.6 %all-reduce.17.cloned.1.call-done = (f32[1024,1024]{1,0:T(8,128)}, f32[1024,1024]{1,0:T(8,128)}) async-done(((f32[1024,1024]{1,0:T(8,128)}, f32[1024,1024]{1,0:T(8,128)}), (f32[1024,1024]{1,0:T(8,128)}, f32[1024,1024]{1,0:T(8,128)})) %all-reduce.17.cloned.1.call-update) | async-done | bytes 8388624 | tf_op jit(solution)/shard_map/psum | solution.py:178
  674.8 19.8 reshape.388
  695.8 330.8 %all-reduce.15.cloned.1.call-done = f32[16,295296]{1,0:T(8,128)} async-done(((f32[16,295296]{1,0:T(8,128)}), f32[16,295296]{1,0:T(8,128)}) %all-reduce.15.cloned.1.call-update) | async-done | bytes 18898960
  1026.6 6.2 dynamic-slice_bitcast_fusion
  1032.8 5.7 add_convert_fusion
  1042.2 89.5 %all-gather.3.cloned.1.call-done = f32[16,1,295296]{2,1,0:T(1,128)} async-done(((f32[1,1,295296]{2,1,0:T(1,128)}), f32[16,1,295296]{2,1,0:T(1,128)}) %all-gather.3.cloned.1.call-update) | async-done | bytes 18898960 | tf_op jit(solution)/shard_map/all_gather | solution.py:312
  1133.1 9.5 fusion.93
  1142.6 201.1 %reduce.10 = f32[16,295296]{1,0:T(8,128)} reduce(f32[16,1,295296]{2,1,0:T(1,128)} %all-gather.3.cloned.1.call-done, f32[]{:T(128)} %constant.197), dimensions={1}, to_apply=%all-gather.reduce_sub_computation | reduce | bytes 37797892 | tf_op jit(solution)/shard_map/all_gather | solution.py:312
  1343.7 18.1 slice.221
  1361.8 17.5 slice.224
  1379.3 17.5 slice.219
  1396.8 1045.8 %slice.227 = f32[1181184,4]{1,0:T(8,128)} reshape(f32[16,295296]{1,0:T(8,128)} %reduce.10) | data formatting | bytes 37797888 | tf_op jit(solution)/shard_map/slice | solution.py:74
  2442.6 4.9 reshape.392
  2447.5 5.2 reshape.391
  2452.7 5.2 reshape.390
  (278 shorter events, 125.7 us)
Async XLA Ops:
  7.2 188.3 %copy-start = (bf16[4,256,1024]{2,1,0:T(8,128)(2,1)S(1)}, bf16[4,256,1024]{2,1,0:T(8,128)(2,1)}, u32[]{:S(2)}) copy-start(bf16[4,256,1024]{2,1,0:T(8,128)(2,1)} %param.40) | copy-start | bytes 6291460
  7.2 5.9 copy-start.64
  7.2 5.9 copy-start.52
  7.2 153.9 %all-reduce.11.cloned.1.call-start = ((), (), s32[]{:S(2)}) async-start(), calls=%async_computation | async-start | bytes 8388608 | tf_op jit(solution)/shard_map/psum | solution.py:149
  7.3 5.9 copy-start.6
  9.5 4.6 copy-start.59
  13.1 9.9 copy-start.46
  14.1 24.4 copy-start.44
  14.6 4.3 copy-start.42
  16.1 6.8 copy-start.39
  38.5 8.6 copy-start.50
  50.5 358.1 %all-reduce.13.cloned.1.call-start = ((), (), s32[]{:S(2)}) async-start(), calls=%async_computation.1 | async-start | bytes 8388608 | tf_op jit(solution)/shard_map/psum | solution.py:215
  108.2 56.4 %copy-start.58 = (f32[1024]{0:T(1024)S(1)}, f32[1024]{0:T(1024)}, u32[]{:S(2)}) copy-start(f32[1024]{0:T(1024)} %param.36) | copy-start | bytes 12292
  184.6 4.8 copy-start.5
  184.6 10.9 slice-start.7
  189.5 6.0 copy-start.68
  189.5 6.0 slice-start.8
  189.5 6.0 slice-start.9
  195.5 5.6 copy-start.21
  222.5 23.5 slice-start.10
  236.4 9.7 slice-start.11
  255.7 4.2 copy-start.13
  259.9 4.6 copy-start.27
  259.9 4.6 copy-start.36
  300.6 365.0 %all-reduce.17.cloned.1.call-start = ((), (), s32[]{:S(2)}) async-start(), calls=%async_computation.4 | async-start | bytes 16777216 | tf_op jit(solution)/shard_map/psum | solution.py:178
  300.6 4.6 copy-start.11
  341.6 5.0 copy-start.22
  355.6 58.8 %copy-start.18 = (bf16[1024,1024]{1,0:T(8,128)(2,1)S(1)}, bf16[1024,1024]{1,0:T(8,128)(2,1)}, u32[]{:S(2)}) copy-start(bf16[1024,1024]{1,0:T(8,128)(2,1)} %param.41) | copy-start | bytes 6291460
  408.6 5.8 copy-start.4
  408.6 9.5 slice-start.5
  424.5 4.8 copy-start.20
  424.5 8.2 slice-start.1
  424.5 8.2 slice-start.2
  424.5 8.2 slice-start.3
  429.4 4.1 slice-start.4
  444.5 11.5 copy-start.32
  447.3 8.7 copy-start.47
  460.3 6.6 copy-start.37
  461.7 5.2 copy-start.29
  466.9 559.7 %all-reduce.15.cloned.1.call-start = ((), (), s32[]{:S(2)}) async-start(), calls=%async_computation.3 | async-start | bytes 37797888
  466.9 4.6 copy-start.9
  466.9 8.1 copy-start.25
  665.6 5.5 copy-start.31
  694.6 437.2 %all-gather.3.cloned.1.call-start = ((), (), s32[]{:S(2)}) async-start(), calls=%async_computation.2 | async-start | bytes 20080128 | tf_op jit(solution)/shard_map/all_gather | solution.py:312
  1032.8 5.7 copy-start.12
  1032.8 6.8 copy-start.15
  2457.9 10.5 copy-start.1
  2461.0 6.5 slice-start
  (38 other events, 87.0 us)
Sparse Core Ops, SparseCore 0:
  50.6 110.5 all-reduce.10
  300.7 107.8 all-reduce.12
  467.0 198.5 all-reduce.16
  694.7 331.8 all-reduce.14
  1032.9 98.8 all-gather.2
where the time goes:
time: 2480 us
  local copies, waits for them, and re-layouts  1310 us (53%)
  waiting for transfers between devices  703 us (28%)
  other arithmetic  321 us (13%)
  matrix products  122 us (5%)
    slice x11, local copies, waits for them, and re-layouts, unpack_rows(): result.append(flattened[offset:offset + member.size].reshape(member.shape))  1120 us
    unnamed x6, waiting for transfers between devices  331 us
    all_gather x1, other arithmetic, per_device(): lax.all_gather(joined_shares, 'dp', axis=0, tiled=True)  201 us
    psum x1, waiting for transfers between devices, per_device(): routed_total = lax.psum(routed_part, 'tensor')  177 us
    all_gather x1, waiting for transfers between devices, per_device(): lax.all_gather(joined_shares, 'dp', axis=0, tiled=True)  89.5 us
    unnamed x180, local copies, waits for them, and re-layouts  53.6 us
    psum x1, waiting for transfers between devices, per_device(): lax.psum((routed_grad_part, gate_pair_part), 'tensor')  53 us
    psum x1, waiting for transfers between devices, per_device(): attn_total = lax.psum(attn_part, 'tensor')  52.9 us
  transfers between devices with their start and end apart: 5, of which 5 were waited for; matrix products, arithmetic and copies ran while one was open for 6% of the time, Pallas kernels for 0%

commit v1 on v0

--- a/solution.py
+++ b/solution.py
@@ -60,20 +60,9 @@
     return jnp.where(allowed, scores, masked_value)
 
 
-def pack_rows(arrays, parts_count):
-    flattened = jnp.concatenate([member.reshape(-1) for member in arrays])
-    padding = -flattened.shape[0] % parts_count
-    return flattened.reshape(parts_count, -1)
-
-
-def unpack_rows(packed, arrays):
-    flattened = packed.reshape(-1)
-    result = []
-    offset = 0
-    for member in arrays:
-        result.append(flattened[offset : offset + member.size].reshape(member.shape))
-        offset = offset + member.size
-    return result
+def pack_grads(parts_count, wide, tall, vectors):
+    rows = jnp.concatenate(wide + tall + [jnp.stack(vectors)], axis=0)
+    return jnp.pad(rows, ((0, -rows.shape[0] % (8 * parts_count)), (0, 0)))
 
 
 def per_device(
@@ -227,7 +216,6 @@
         grad_input_two, normed_two, inverse_two, norm_gain_two
     )
     grad_middle = grad_top + grad_middle_norm
-    expert_bucket = [grad_wgate, grad_wup, grad_wdown, grad_router, grad_gain_two]
     grad_attn = grad_middle.astype(jnp.bfloat16)
     grad_wout = jnp.einsum("tn,td->nd", attended, grad_attn, preferred_element_type=jnp.float32)
     grad_heads = (
@@ -304,25 +292,46 @@
         input_grad_one, normed_one, inverse_one, norm_gain_one
     )
     grad_input = grad_middle + grad_resid_norm
-    attention_bucket = [grad_gain_one, grad_wquery, grad_wkey, grad_wvalue, grad_wout]
-    joined = expert_bucket + attention_bucket
-    joined_shares = lax.psum_scatter(
-        pack_rows(joined, parts_count), "dp", scatter_dimension=0, tiled=True
-    )
-    summed = unpack_rows(lax.all_gather(joined_shares, "dp", axis=0, tiled=True), joined)
+    gate_wide = jnp.concatenate([grad_wgate[e] for e in range(EXPERTS)], axis=1)
+    up_wide = jnp.concatenate([grad_wup[e] for e in range(EXPERTS)], axis=1)
+    qkv_wide = jnp.concatenate([grad_wquery, grad_wkey, grad_wvalue], axis=1)
+    hidden_part = w_down.shape[1]
+    down_rows = grad_wdown.reshape(EXPERTS * hidden_part, D)
+    packed = pack_grads(
+        parts_count,
+        [gate_wide, up_wide, qkv_wide],
+        [down_rows, grad_wout],
+        [grad_gain_one, grad_gain_two] + [grad_router[:, e] for e in range(EXPERTS)],
+    )
+    shares = lax.psum_scatter(packed, "dp", scatter_dimension=0, tiled=True)
+    total = lax.all_gather(shares, "dp", axis=0, tiled=True)
+    split = [hidden_part * e for e in range(EXPERTS + 1)]
+    sum_gate = jnp.stack([total[:D, split[e] : split[e + 1]] for e in range(EXPERTS)])
+    sum_up = jnp.stack([total[D : 2 * D, split[e] : split[e + 1]] for e in range(EXPERTS)])
+    q_cols = w_query.shape[1]
+    kv_cols = w_key.shape[1]
+    sum_query = total[2 * D : 3 * D, :q_cols]
+    sum_key = total[2 * D : 3 * D, q_cols : q_cols + kv_cols]
+    sum_value = total[2 * D : 3 * D, q_cols + kv_cols : q_cols + 2 * kv_cols]
+    at = 3 * D
+    sum_down = total[at : at + EXPERTS * hidden_part].reshape(w_down.shape)
+    at += EXPERTS * hidden_part
+    sum_out = total[at : at + w_out.shape[0]]
+    at += w_out.shape[0]
+    small = total[at : at + 2 + EXPERTS]
     return (
         block_out,
         grad_input,
-        summed[5],
-        summed[6],
-        summed[7],
-        summed[8],
-        summed[9],
-        summed[4],
-        summed[3],
-        summed[0],
-        summed[1],
-        summed[2],
+        small[0],
+        sum_query,
+        sum_key,
+        sum_value,
+        sum_out,
+        small[1],
+        small[2 : 2 + EXPERTS].T,
+        sum_gate,
+        sum_up,
+        sum_down,
     )
 
 

time: 2480 us -> 1050 us (0.42)
  local copies, waits for them, and re-layouts: 1310 us -> 204 us
  other arithmetic: 321 us -> 132 us
  waiting for transfers between devices: 703 us -> 569 us
    slice x11 -> x4, local copies, waits for them, and re-layouts: 1120 us -> 12.6 us  [the longest x1 4.79 us: per_device(): sum_down = total[at:at + EXPERTS * hidden_part].reshape(w_down.shape)]
    unnamed x6 -> x5, waiting for transfers between devices: 331 us -> 0.08 us
    all_gather x1 -> x0, other arithmetic: 201 us -> none  [per_device(): lax.all_gather(joined_shares, 'dp', axis=0, tiled=True)]
    reduce_scatter x0 -> x1, waiting for transfers between devices: none -> 199 us  [per_device(): shares = lax.psum_scatter(packed, 'dp', scatter_dimension=0, tiled=True)]
    reshape x5 -> x1, local copies, waits for them, and re-layouts: 36.4 us -> 5.49 us  [per_device(): down_rows = grad_wdown.reshape(EXPERTS * hidden_part, D)]
    unnamed x180 -> x160, local copies, waits for them, and re-layouts: 53.6 us -> 35.4 us
  transfers between devices with their start and end apart: 5 -> 5, of which waited for: 5 -> 5; matrix products, arithmetic and copies ran while one was open for 6% -> 14% of each run, Pallas kernels for 0% -> 0%
where the time goes in v1:
time: 1050 us; the launch traced here: 1040 us
  waiting for transfers between devices  569 us (54%)
  local copies, waits for them, and re-layouts  204 us (19%)
  other arithmetic  132 us (13%)
  matrix products  117 us (11%)
  between operations  15.3 us (1%)
    reduce_scatter x1, waiting for transfers between devices, per_device(): shares = lax.psum_scatter(packed, 'dp', scatter_dimension=0, tiled=True)  199 us
    psum x1, waiting for transfers between devices, per_device(): routed_total = lax.psum(routed_part, 'tensor')  154 us
    all_gather x1, waiting for transfers between devices, per_device(): total = lax.all_gather(shares, 'dp', axis=0, tiled=True)  92.6 us
    psum x1, waiting for transfers between devices, per_device(): lax.psum((routed_grad_part, gate_pair_part), 'tensor')  68.8 us
    psum x1, waiting for transfers between devices, per_device(): attn_total = lax.psum(attn_part, 'tensor')  53.5 us
    unnamed x160, local copies, waits for them, and re-layouts  35.4 us
    scatter-add x1, other arithmetic, per_device(): routed_part = jnp.zeros((length + 1, D), jnp.float32).at[slot_token].add(...  25.6 us
    scatter-add x1, other arithmetic, per_device(): jnp.zeros((length + 1, D), jnp.float32).at[slot_token].add(grad_rows)  25.5 us
  transfers between devices with their start and end apart: 5, of which 5 were waited for; matrix products, arithmetic and copies ran while one was open for 14% of the time, Pallas kernels for 0%

profile of v1, /device:TPU:0, one launch (start us, length us, event | category | flops | bytes accessed | tf_op | source)
XLA Modules:
  0.0 1043.2 jit_solution(16456109151212319496)
XLA Ops:
  23.0 7.5 fusion.101
  30.5 8.0 fusion.3
  38.5 7.5 fusion.61
  47.1 3.3 fusion.103
  51.1 11.8 %gather_fusion = s32[2048]{0:T(1024)S(1)} fusion(s32[2048]{0:T(1024)S(1)} %reshape.323, s32[2048]{0:T(1024)S(1)} %broadcast_clamp_fusion), kind=kCustom, calls=%fused_computation | custom fusion | bytes 24576 | tf_op jit(solution)/shard_map/gather | solution.py:37
  64.6 8.0 scatter_custom_fusion
  72.7 8.1 scatter_custom_fusion.1
  80.8 8.1 scatter_custom_fusion.2
  88.9 4.1 concatenate.38
  93.0 14.6 %gather_fusion.3 = f32[2560,1024]{1,0:T(8,128)} fusion(f32[1025,1024]{1,0:T(8,128)} %concatenate.38, s32[3072]{0:T(1024)S(1)} %pad_clamp_fusion), kind=kCustom, calls=%fused_computation.3 | custom fusion | bytes 20981760 | tf_op jit(solution)/shard_map/gather | solution.py:171
  107.7 53.5 %all-reduce.10.cloned.1.call-done = f32[1024,1024]{1,0:T(8,128)} async-done(((f32[1024,1024]{1,0:T(8,128)}), f32[1024,1024]{1,0:T(8,128)}) %all-reduce.10.cloned.1.call-update) | async-done | bytes 4194320 | tf_op jit(solution)/shard_map/psum | solution.py:138
  161.2 3.5 multiply_reduce_fusion.3
  170.6 13.9 %gather_fusion.2 = bf16[2560,1024]{1,0:T(8,128)(2,1)} fusion(bf16[1025,1024]{1,0:T(8,128)(2,1)} %concatenate.37, s32[3072]{0:T(1024)S(1)} %pad_clamp_fusion), kind=kCustom, calls=%fused_computation.2 | custom fusion | bytes 10496000 | tf_op jit(solution)/shard_map/gather | solution.py:150
  184.5 4.8 fusion.105
  189.4 6.0 multiply_convert_fusion.4
  195.4 5.6 multiply_reduce_fusion
  201.1 15.1 %scatter_custom_fusion.5 = f32[2049]{0:T(1024)S(1)} fusion(s32[2560]{0:T(1024)S(1)} %compare_select_fusion.1, f32[2560]{0:T(1024)S(1)} %reshape.410, f32[]{:T(128)} %constant.163.clone.1), kind=kCustom, calls=%fused_computation.164 | custom fusion | flops 2560 | bytes 8200 | tf_op jit(solution)/shard_map/scatter-add | solution.py:177
  216.9 5.0 psum.38
  222.4 13.8 %gather_fusion.1 = f32[2560]{0:T(1024)S(1)} fusion(f32[2049]{0:T(1024)S(1)} %pad_maximum_fusion.7, s32[3072]{0:T(1024)S(1)} %pad_clamp_fusion.1), kind=kCustom, calls=%fused_computation.1 | custom fusion | bytes 30720 | tf_op jit(solution)/shard_map/gather | solution.py:153
  236.3 8.2 multiply_convert_fusion.2
  247.0 5.5 convolution_add_fusion
  252.5 25.5 %scatter_custom_fusion.4 = f32[1025,1024]{1,0:T(8,128)} fusion(s32[2560]{0:T(1024)S(1)} %compare_select_fusion.2, f32[2560,1024]{1,0:T(8,128)} %bitcast.263, f32[]{:T(128)} %constant.163.clone.1), kind=kCustom, calls=%fused_computation.74 | custom fusion | flops 2621440 | bytes 4198912 | tf_op jit(solution)/shard_map/scatter-add | solution.py:202
  278.0 4.8 slice.307
  282.9 8.8 bitcast_multiply_fusion.1
  291.6 25.6 %scatter_custom_fusion.3 = f32[1025,1024]{1,0:T(8,128)} fusion(s32[2560]{0:T(1024)S(1)} %compare_select_fusion.2, f32[2560,1024]{1,0:T(8,128)} %bitcast_multiply_fusion.1, f32[]{:T(128)} %constant.163.clone.1), kind=kCustom, calls=%fused_computation.76 | custom fusion | flops 2621440 | bytes 4198912 | tf_op jit(solution)/shard_map/scatter-add | solution.py:165
  317.2 4.8 slice.306
  322.1 68.8 %all-reduce.12.cloned.1.call-done = f32[1024,1024]{1,0:T(8,128)} async-done(((f32[1024,1024]{1,0:T(8,128)}), f32[1024,1024]{1,0:T(8,128)}) %all-reduce.12.cloned.1.call-update) | async-done | bytes 4194320 | tf_op jit(solution)/shard_map/psum | solution.py:204
  390.9 5.8 multiply_reduce_fusion.1
  402.1 5.1 fusion.7
  407.2 4.8 fusion.9
  416.1 8.1 fusion
  429.9 8.5 fusion.2
  445.8 3.3 add_add_fusion
  450.5 8.0 fusion.35
  458.5 5.5 copy.146
  468.5 4.3 fusion.109
  493.6 154.3 %all-reduce.14.cloned.1.call-done = (f32[1024,1024]{1,0:T(8,128)}, f32[1024,1024]{1,0:T(8,128)}) async-done(((f32[1024,1024]{1,0:T(8,128)}, f32[1024,1024]{1,0:T(8,128)}), (f32[1024,1024]{1,0:T(8,128)}, f32[1024,1024]{1,0:T(8,128)})) %all-reduce.14.cloned.1.call-update) | async-done | bytes 8388624 | tf_op jit(solution)/shard_map/psum | solution.py:167
  647.9 3.3 fusion.23
  652.2 21.8 %concatenate.43 = f32[4614,1024]{0,1:T(8,128)} concatenate(f32[1024,1024]{0,1:T(8,128)} %pad_maximum_fusion, f32[1024,1024]{0,1:T(8,128)} %pad_maximum_fusion.1, f32[1024,1024]{0,1:T(8,128)} %pad_maximum_fusion.2, f32[1024,1024]{0,1:T(8,128)} %copy.146, f32[512,1024]{0,1:T(8,128)} %fusion.63, f32[1,1024]{0,1:T(8,128)} %copy.119, f32[1,1024]{0,1:T(8,128)} %copy.120, ...), dimensions={0} | concatenate | bytes 37797888 | tf_op jit(solution)/shard_map/concatenate | solution.py:64
  674.0 19.5 %copy.149 = f32[4614,1024]{1,0:T(8,128)} copy(f32[4614,1024]{0,1:T(8,128)} %concatenate.43) | data formatting | bytes 37797888
  693.5 16.2 %pad.18.clone = f32[4736,1024]{1,0:T(8,128)} pad(f32[4614,1024]{1,0:T(8,128)} %copy.149, f32[]{:T(128)} %constant.163.clone.1), padding=0_122x0_0 | pad | bytes 38297604 | tf_op jit(solution)/shard_map/jit(_pad)/pad | solution.py:65
  709.9 199.3 %reduce-scatter.4.cloned.1.call-done = f32[296,1024]{1,0:T(8,128)} async-done(((f32[4736,1024]{1,0:T(8,128)}), f32[296,1024]{1,0:T(8,128)}) %reduce-scatter.4.cloned.1.call-update) | async-done | bytes 1212432 | tf_op jit(solution)/shard_map/reduce_scatter | solution.py:306
  909.2 5.7 add_convert_fusion
  918.5 92.6 %all-gather.2.cloned.1.call-done = f32[4736,1024]{1,0:T(8,128)} async-done(((f32[296,1024]{1,0:T(8,128)}), f32[4736,1024]{1,0:T(8,128)}) %all-gather.2.cloned.1.call-update) | async-done | bytes 19398672 | tf_op jit(solution)/shard_map/all_gather | solution.py:307
  1011.2 6.6 slice_bitcast_fusion.3
  1025.2 3.2 slice.327
  1028.4 3.2 slice.324
  1031.6 4.8 slice.338
  (263 shorter events, 90.0 us)
Async XLA Ops:
  7.2 188.2 %copy-start = (bf16[4,256,1024]{2,1,0:T(8,128)(2,1)S(1)}, bf16[4,256,1024]{2,1,0:T(8,128)(2,1)}, u32[]{:S(2)}) copy-start(bf16[4,256,1024]{2,1,0:T(8,128)(2,1)} %param.40) | copy-start | bytes 6291460
  7.2 5.9 copy-start.64
  7.2 5.9 copy-start.51
  7.2 154.0 %all-reduce.10.cloned.1.call-start = ((), (), s32[]{:S(2)}) async-start(), calls=%async_computation.1 | async-start | bytes 8388608 | tf_op jit(solution)/shard_map/psum | solution.py:138
  7.3 5.9 copy-start.9
  9.5 4.6 copy-start.59
  13.1 9.9 copy-start.45
  14.1 24.4 %copy-start.43 = (bf16[1024,256]{0,1:T(8,128)(2,1)}, bf16[1024,256]{0,1:T(8,128)(2,1)S(1)}, u32[]{:S(2)}) copy-start(bf16[1024,256]{0,1:T(8,128)(2,1)S(1)} %convolution_convert_fusion.3) | copy-start | bytes 1572868
  14.6 4.3 copy-start.41
  16.1 6.8 copy-start.38
  38.5 8.6 copy-start.49
  50.4 340.4 %all-reduce.12.cloned.1.call-start = ((), (), s32[]{:S(2)}) async-start(), calls=%async_computation.2 | async-start | bytes 8388608 | tf_op jit(solution)/shard_map/psum | solution.py:204
  107.7 57.0 %copy-start.58 = (f32[1024]{0:T(1024)S(1)}, f32[1024]{0:T(1024)}, u32[]{:S(2)}) copy-start(f32[1024]{0:T(1024)} %param.36) | copy-start | bytes 12292
  184.5 4.8 copy-start.5
  184.5 10.9 %slice-start.6 = ((s8[10485760]{0:T(1024)(128)(4,1)}), s8[4194304]{0:T(1024)(128)(4,1)S(1)}, s32[]{:S(2)}) async-start(s8[10485760]{0:T(1024)(128)(4,1)} %bitcast.251), calls=%async_computation.12 | async-start | bytes 8388608
  189.4 6.0 copy-start.67
  189.4 6.0 slice-start.7
  189.4 6.0 slice-start.8
  195.4 5.7 copy-start.20
  236.2 8.2 copy-start.56
  236.3 8.2 copy-start.26
  282.8 365.1 %all-reduce.14.cloned.1.call-start = ((), (), s32[]{:S(2)}) async-start(), calls=%async_computation.5 | async-start | bytes 16777216 | tf_op jit(solution)/shard_map/psum | solution.py:167
  322.0 74.6 %copy-start.17 = (bf16[1024,1024]{1,0:T(8,128)(2,1)S(1)}, bf16[1024,1024]{1,0:T(8,128)(2,1)}, u32[]{:S(2)}) copy-start(bf16[1024,1024]{1,0:T(8,128)(2,1)} %param.41) | copy-start | bytes 6291460
  390.9 5.8 copy-start.4
  390.9 9.7 slice-start.4
  396.7 4.0 slice-start.5
  407.1 4.9 copy-start.19
  407.1 8.2 slice-start
  407.1 8.2 slice-start.1
  407.2 8.2 slice-start.2
  412.0 4.1 slice-start.3
  427.0 11.3 %copy-start.29 = (bf16[1024,4,64]{0,2,1:T(8,128)(2,1)}, bf16[1024,4,64]{0,2,1:T(8,128)(2,1)S(1)}, u32[]{:S(2)}) copy-start(bf16[1024,4,64]{0,2,1:T(8,128)(2,1)S(1)} %fusion.46) | copy-start | bytes 1572868
  429.9 8.5 copy-start.46
  442.6 6.5 copy-start.36
  444.0 5.2 copy-start.27
  449.2 460.0 %reduce-scatter.4.cloned.1.call-start = ((), (), s32[]{:S(2)}) async-start(), calls=%async_computation.4 | async-start | bytes 20611072 | tf_op jit(solution)/shard_map/reduce_scatter | solution.py:306
  458.4 5.5 copy-start.12
  463.9 4.6 copy-start.23
  473.5 4.1 copy-start.25
  480.0 3.7 copy-start.10
  486.9 3.8 copy-start.7
  486.9 4.1 copy-start.16
  493.6 158.6 %copy-start.33 = (f32[1,1024]{0,1:T(8,128)S(1)}, f32[1,1024]{0,1:T(8,128)}, u32[]{:S(2)}) copy-start(f32[1,1024]{0,1:T(8,128)} %copy.124) | copy-start | bytes 12292
  493.6 158.6 %copy-start.34 = (f32[1,1024]{0,1:T(8,128)S(1)}, f32[1,1024]{0,1:T(8,128)}, u32[]{:S(2)}) copy-start(f32[1,1024]{0,1:T(8,128)} %copy.123) | copy-start | bytes 12292
  709.8 301.4 %all-gather.2.cloned.1.call-start = ((), (), s32[]{:S(2)}) async-start(), calls=%async_computation.3 | async-start | bytes 20611072 | tf_op jit(solution)/shard_map/all_gather | solution.py:307
  909.2 5.7 copy-start.8
  909.2 6.7 copy-start.14
  1028.4 8.0 copy-start.1
  (36 other events, 81.7 us)
Sparse Core Ops, SparseCore 0:
  50.6 110.5 all-reduce.9
  282.9 107.8 all-reduce.11
  449.3 198.5 all-reduce.13
  709.9 199.1 reduce-scatter.3
  910.6 100.5 all-gather.1

commit v2 on v0

v2 whole, which is shorter than its diff:
```python
import functools

import jax
import jax.numpy as jnp
from jax import lax
from jax.experimental import pallas as pl
from jax.experimental.pallas import tpu as pltpu
from jax.sharding import PartitionSpec as P

D = 1024
HEAD_DIM = 64
EXPERTS = 4
TOPK = 2
CAP = 640
MOST = 512
ROWS8 = 8

norm_eps = 1e-05
masked_value = -1e30
f32 = jnp.float32
bf16 = jnp.bfloat16
i32 = jnp.int32

NN = (((1,), (0,)), ((), ()))
NT = (((1,), (1,)), ((), ()))
TN = (((0,), (0,)), ((), ()))


def mm(left, right, dims=NN):
    return lax.dot_general(left, right, dims, preferred_element_type=f32)


def full_spec(shape):
    zeros = (0,) * len(shape)
    return pl.BlockSpec(shape, lambda *_: zeros, pipeline_mode=pl.Buffered(1))


def route_kernel(choice_ref, order_ref, slot_ref):
    length = choice_ref.shape[1]
    pairs = 2 * length
    order = order_ref[...]
    where_pair = (order & 1) * length + (order >> 1)
    match = (lax.broadcasted_iota(i32, (pairs, pairs), 0) == where_pair).astype(f32).astype(bf16)
    experts = lax.broadcasted_iota(i32, (ROWS8, length), 0)
    first = (choice_ref[0:1, :] == experts).astype(f32)
    second = (choice_ref[1:2, :] == experts).astype(f32)
    hot = jnp.concatenate([first, second], axis=1)
    ordered = mm(hot.astype(bf16), match)
    step = 512
    tri = (
        lax.broadcasted_iota(i32, (step, step), 0) < lax.broadcasted_iota(i32, (step, step), 1)
    ).astype(f32)
    carry = jnp.zeros((ROWS8, 1), f32)
    ranks = []
    for begin in range(0, pairs, step):
        part = ordered[:, begin : begin + step]
        inside = mm(part.astype(bf16), tri.astype(bf16)) + carry
        ranks.append(jnp.sum(inside * part, axis=0, keepdims=True))
        carry = carry + jnp.sum(part, axis=1, keepdims=True)
    rank = jnp.concatenate(ranks, axis=1)
    high = jnp.floor(rank * (1.0 / 64.0))
    low_part = rank - 64.0 * high
    row_id = lax.broadcasted_iota(i32, (ROWS8, pairs), 0)
    both = jnp.where(row_id == 0, high, jnp.where(row_id == 1, low_part, 0.0))
    back = mm(both.astype(bf16), match, NT)
    slot = (64.0 * back[0:1, :] + back[1:2, :]).astype(i32)
    slot_ref[...] = jnp.where(
        first > 0.5, slot[:, :length], jnp.where(second > 0.5, slot[:, length:], -1)
    )


def route(choice_t, order):
    length = choice_t.shape[1]
    return pl.pallas_call(
        route_kernel,
        out_shape=jax.ShapeDtypeStruct((ROWS8, length), i32),
        compiler_params=pltpu.CompilerParams(vmem_limit_bytes=50 << 20),
        name="route",
    )(choice_t, order)


def attn_blocks(length, rows):
    blocks = []
    for begin in range(0, length, rows):
        start = max(0, begin + rows - MOST - rows)
        start = max(0, (begin + 1 - MOST) // 128 * 128)
        blocks.append((begin, start, begin + rows))
    return blocks


def attn_fwd_kernel(rows, q_ref, k_ref, v_ref, segc_ref, segr_ref, o_ref):
    length = q_ref.shape[0]
    for begin, start, stop in attn_blocks(length, rows):
        wide = stop - start
        row_pos = begin + lax.broadcasted_iota(i32, (rows, wide), 0)
        col_pos = start + lax.broadcasted_iota(i32, (rows, wide), 1)
        allowed = (segc_ref[begin:stop, :] == segr_ref[:, start:stop]) & (col_pos <= row_pos)
        bias = jnp.where(allowed, 0.0, masked_value)
        bias = jnp.concatenate([bias, bias], axis=0)
        for kv in range(2):
            lo = kv * HEAD_DIM
            q_two = jnp.concatenate(
                [
                    q_ref[begin:stop, 2 * lo : 2 * lo + HEAD_DIM],
                    q_ref[begin:stop, 2 * lo + HEAD_DIM : 2 * lo + 2 * HEAD_DIM],
                ],
                axis=0,
            )
            q_two = q_two * jnp.asarray(HEAD_DIM**-0.5, bf16)
            scores = mm(q_two, k_ref[start:stop, lo : lo + HEAD_DIM], NT) + bias
            peak = jnp.max(scores, axis=1, keepdims=True)
            raised = jnp.exp(scores - peak)
            total = jnp.sum(raised, axis=1, keepdims=True)
            probs = (raised * (1.0 / total)).astype(bf16)
            out = mm(probs, v_ref[start:stop, lo : lo + HEAD_DIM])
            out = out.astype(bf16).astype(f32)
            o_ref[begin:stop, 2 * lo : 2 * lo + 2 * HEAD_DIM] = jnp.concatenate(
                [out[:rows], out[rows:]], axis=1
            )


def attn_fwd(qkv, seg_col, seg_row, q_cols):
    length = qkv.shape[0]
    pairs = q_cols // 256
    return pl.pallas_call(
        functools.partial(attn_fwd_kernel, 256),
        grid=(pairs,),
        in_specs=[
            pl.BlockSpec((length, 256), lambda g: (0, g)),
            pl.BlockSpec((length, 128), lambda g: (0, 2 * pairs + g)),
            pl.BlockSpec((length, 128), lambda g: (0, 3 * pairs + g)),
            full_spec((length, 1)),
            full_spec((1, length)),
        ],
        out_specs=pl.BlockSpec((length, 256), lambda g: (0, g)),
        out_shape=jax.ShapeDtypeStruct((length, q_cols), f32),
        compiler_params=pltpu.CompilerParams(vmem_limit_bytes=50 << 20),
        name="attn_fwd",
    )(qkv, qkv, qkv, seg_col, seg_row)


def attn_bwd_kernel(
    rows, q_ref, k_ref, v_ref, do_ref, segc_ref, segr_ref, dq_ref, dk_ref, dv_ref, dks, dvs
):
    length = q_ref.shape[0]
    scale = HEAD_DIM**-0.5
    dks[...] = jnp.zeros_like(dks)
    dvs[...] = jnp.zeros_like(dvs)
    for begin, start, stop in attn_blocks(length, rows):
        wide = stop - start
        row_pos = begin + lax.broadcasted_iota(i32, (wide, rows), 1)
        col_pos = start + lax.broadcasted_iota(i32, (wide, rows), 0)
        allowed = (segr_ref[:, begin:stop] == segc_ref[start:stop, :]) & (col_pos <= row_pos)
        bias = jnp.where(allowed, 0.0, masked_value)
        bias = jnp.concatenate([bias, bias], axis=1)
        for kv in range(2):
            lo = kv * HEAD_DIM
            q_two = jnp.concatenate(
                [
                    q_ref[begin:stop, 2 * lo : 2 * lo + HEAD_DIM],
                    q_ref[begin:stop, 2 * lo + HEAD_DIM : 2 * lo + 2 * HEAD_DIM],
                ],
                axis=0,
            )
            q_two = q_two * jnp.asarray(scale, bf16)
            do_two = jnp.concatenate(
                [
                    do_ref[begin:stop, 2 * lo : 2 * lo + HEAD_DIM],
                    do_ref[begin:stop, 2 * lo + HEAD_DIM : 2 * lo + 2 * HEAD_DIM],
                ],
                axis=0,
            )
            k_win = k_ref[start:stop, lo : lo + HEAD_DIM]
            v_win = v_ref[start:stop, lo : lo + HEAD_DIM]
            scores = mm(k_win, q_two, NT) + bias
            peak = jnp.max(scores, axis=0, keepdims=True)
            raised = jnp.exp(scores - peak)
            total = jnp.sum(raised, axis=0, keepdims=True)
            probs = raised * (1.0 / total)
            grad_probs = mm(v_win, do_two, NT)
            row_dot = jnp.sum(probs * grad_probs, axis=0, keepdims=True)
            grad_scores = (probs * (grad_probs - row_dot)).astype(bf16)
            dvs[start:stop, lo : lo + HEAD_DIM] += mm(probs.astype(bf16), do_two)
            dks[start:stop, lo : lo + HEAD_DIM] += mm(grad_scores, q_two)
            dq = (mm(grad_scores, k_win, TN) * scale).astype(bf16)
            dq_ref[begin:stop, 2 * lo : 2 * lo + 2 * HEAD_DIM] = jnp.concatenate(
                [dq[:rows], dq[rows:]], axis=1
            )
    dk_ref[...] = dks[...].astype(bf16)
    dv_ref[...] = dvs[...].astype(bf16)


def attn_bwd(qkv, grad_heads, seg_col, seg_row, q_cols):
    length = qkv.shape[0]
    pairs = q_cols // 256
    return pl.pallas_call(
        functools.partial(attn_bwd_kernel, 256),
        grid=(pairs,),
        in_specs=[
            pl.BlockSpec((length, 256), lambda g: (0, g)),
            pl.BlockSpec((length, 128), lambda g: (0, 2 * pairs + g)),
            pl.BlockSpec((length, 128), lambda g: (0, 3 * pairs + g)),
            pl.BlockSpec((length, 256), lambda g: (0, g)),
            full_spec((length, 1)),
            full_spec((1, length)),
        ],
        out_specs=[
            pl.BlockSpec((length, 256), lambda g: (0, g)),
            pl.BlockSpec((length, 128), lambda g: (0, g)),
            pl.BlockSpec((length, 128), lambda g: (0, g)),
        ],
        out_shape=[
            jax.ShapeDtypeStruct((length, q_cols), bf16),
            jax.ShapeDtypeStruct((length, q_cols // 2), bf16),
            jax.ShapeDtypeStruct((length, q_cols // 2), bf16),
        ],
        scratch_shapes=[pltpu.VMEM((length, 128), f32), pltpu.VMEM((length, 128), f32)],
        compiler_params=pltpu.CompilerParams(vmem_limit_bytes=50 << 20),
        name="attn_bwd",
    )(qkv, qkv, qkv, grad_heads, seg_col, seg_row)


def moe_kernel(
    h_s,
    g2_ref,
    wr_ref,
    slotr_ref,
    slotc_ref,
    dy_ref,
    wg_ref,
    wu_ref,
    wd_ref,
    wgx_ref,
    wux_ref,
    wdx_ref,
    out_ref,
    dh_ref,
    dwg_ref,
    dwu_ref,
    dwd_ref,
    small_ref,
    xn_s,
    moe_s,
    gate_s,
    dgate_s,
):
    e = pl.program_id(0)
    length = h_s.shape[0]
    chunk = 256

    @pl.when(e == 0)
    def _():
        def start_rows(c, _):
            rows = pl.ds(pl.multiple_of(c * chunk, chunk), chunk)
            h1 = h_s[rows, :]
            inverse = lax.rsqrt(jnp.mean(h1 * h1, axis=1, keepdims=True) + norm_eps)
            xn_s[rows, :] = (h1 * inverse * g2_ref[...]).astype(bf16)
            return 0

        lax.fori_loop(0, length // chunk, start_rows, 0)
        moe_s[...] = jnp.zeros_like(moe_s)
        dh_ref[...] = jnp.zeros_like(dh_ref)
        dgate_s[...] = jnp.zeros_like(dgate_s)
        logits = mm(wr_ref[...].astype(bf16), xn_s[...], NT)
        chosen = slotr_ref[...] >= 0
        logits = jnp.where(chosen, logits, masked_value)
        peak = jnp.max(logits, axis=0, keepdims=True)
        raised = jnp.where(chosen, jnp.exp(logits - peak), 0.0)
        gate_s[...] = raised / jnp.sum(raised, axis=0, keepdims=True)

    xn = xn_s[...]
    slot_row = slotr_ref[pl.ds(e, 1), :]
    mask = lax.broadcasted_iota(i32, (CAP, length), 0) == slot_row
    place = mask.astype(f32).astype(bf16)
    lane8 = lax.broadcasted_iota(i32, (length, ROWS8), 1)
    slot_col = jnp.sum(jnp.where(lane8 == e, slotc_ref[...], 0), axis=1, keepdims=True)
    place_t = (lax.broadcasted_iota(i32, (length, CAP), 1) == slot_col).astype(f32).astype(bf16)
    gate = jnp.sum(jnp.where(mask, gate_s[pl.ds(e, 1), :], 0.0), axis=1, keepdims=True)
    rows_in = mm(place, xn).astype(bf16)
    dy_slot = mm(place, dy_ref[...])
    dy_gated = (gate * dy_slot).astype(bf16)

    halves = []
    y = None
    for own in (True, False):
        wg = wg_ref[0] if own else wgx_ref[...].astype(bf16)
        wu = wu_ref[0] if own else wux_ref[...].astype(bf16)
        wd = wd_ref[0] if own else wdx_ref[...].astype(bf16)
        g = mm(rows_in, wg)
        u = mm(rows_in, wu)
        sig = 1.0 / (1.0 + jnp.exp(-g))
        act = g * sig
        hid = (act * u).astype(bf16)
        part = mm(hid, wd)
        y = part if y is None else y + part
        dhid = mm(dy_gated, wd, NT)
        dg = (dhid * u * sig * (1.0 + g * (1.0 - sig))).astype(bf16)
        du = (dhid * act).astype(bf16)
        dx = mm(dg, wg, NT) + mm(du, wu, NT)
        halves.append(dx)
        if own:
            dwd_ref[...] = mm(hid, dy_gated, TN)
            dwg_ref[...] = mm(rows_in, dg, TN)
            dwu_ref[...] = mm(rows_in, du, TN)
    dgate_slot = jnp.sum(dy_slot * y, axis=1, keepdims=True)
    dgate_s[pl.ds(e, 1), :] = jnp.sum(jnp.where(mask, dgate_slot, 0.0), axis=0, keepdims=True)
    moe_s[...] += mm(place_t, (gate * y).astype(bf16))
    dh_ref[...] += mm(place_t, (halves[0] + halves[1]).astype(bf16))

    @pl.when(e == EXPERTS - 1)
    def _():
        gates = gate_s[...]
        dgates = dgate_s[...]
        dsel = gates * (dgates - jnp.sum(gates * dgates, axis=0, keepdims=True))
        dlog = dsel.astype(bf16)
        drouter = mm(dlog, xn_s[...])
        wr = wr_ref[...].astype(bf16)
        dlog_t = dsel.T.astype(bf16)
        small_ref[...] = jnp.zeros_like(small_ref)
        small_ref[0:EXPERTS, :] = drouter[0:EXPERTS, :]

        def end_rows(c, total):
            rows = pl.ds(pl.multiple_of(c * chunk, chunk), chunk)
            h1 = h_s[rows, :]
            inverse = lax.rsqrt(jnp.mean(h1 * h1, axis=1, keepdims=True) + norm_eps)
            n2 = h1 * inverse
            out_ref[rows, :] = (h1 + moe_s[rows, :]).astype(bf16)
            return total

        lax.fori_loop(0, length // chunk, end_rows, 0)
        gain = jnp.zeros((1, D), f32)
        for c in range(length // chunk):
            rows = slice(c * chunk, (c + 1) * chunk)
            h1 = h_s[rows, :]
            inverse = lax.rsqrt(jnp.mean(h1 * h1, axis=1, keepdims=True) + norm_eps)
            n2 = h1 * inverse
            dxn = dh_ref[rows, :] + mm(dlog_t[rows, :], wr)
            gain = gain + jnp.sum(dxn * n2, axis=0, keepdims=True)
            scaled = dxn * g2_ref[...]
            mean_term = jnp.mean(scaled * n2, axis=1, keepdims=True)
            dh_ref[rows, :] = dy_ref[rows, :].astype(f32) + inverse * (scaled - n2 * mean_term)
        small_ref[EXPERTS : EXPERTS + 1, :] = gain


def out_kernel(x_ref, oa_ref, ob_ref, wo_ref, wox_ref, h_ref):
    h_ref[...] = x_ref[...].astype(f32) + (
        mm(oa_ref[...].astype(bf16), wo_ref[...])
        + mm(ob_ref[...].astype(bf16), wox_ref[...].astype(bf16))
    )


def out_project(x, oa, ob, wo, other, at):
    length, q_cols = oa.shape
    rows = 256
    return pl.pallas_call(
        out_kernel,
        grid=(length // rows,),
        in_specs=[
            pl.BlockSpec((rows, D), lambda i: (i, 0)),
            pl.BlockSpec((rows, q_cols), lambda i: (i, 0)),
            pl.BlockSpec((rows, q_cols), lambda i: (i, 0)),
            full_spec((q_cols, D)),
            pl.BlockSpec((q_cols, D), lambda i: (at, 0), pipeline_mode=pl.Buffered(1)),
        ],
        out_specs=pl.BlockSpec((rows, D), lambda i: (i, 0)),
        out_shape=jax.ShapeDtypeStruct((length, D), f32),
        name="out_project",
    )(x, oa, ob, wo, other)


def moe(h1, other, g2, wr_t, slot_row, slot_col, dy, w_gate, w_up, w_down):
    length = h1.shape[0]
    hid = w_down.shape[1]
    wide = EXPERTS * hid
    down_at = 2 * D // hid
    return pl.pallas_call(
        moe_kernel,
        grid=(EXPERTS,),
        in_specs=[
            full_spec((length, D)),
            full_spec((1, D)),
            full_spec((ROWS8, D)),
            full_spec((ROWS8, length)),
            full_spec((length, ROWS8)),
            full_spec((length, D)),
            pl.BlockSpec((1, D, hid), lambda e: (e, 0, 0)),
            pl.BlockSpec((1, D, hid), lambda e: (e, 0, 0)),
            pl.BlockSpec((1, hid, D), lambda e: (e, 0, 0)),
            pl.BlockSpec((D, hid), lambda e: (0, e)),
            pl.BlockSpec((D, hid), lambda e: (1, e)),
            pl.BlockSpec((hid, D), lambda e: (down_at + e, 0)),
        ],
        out_specs=[
            full_spec((length, D)),
            full_spec((length, D)),
            pl.BlockSpec((D, hid), lambda e: (0, e)),
            pl.BlockSpec((D, hid), lambda e: (0, e)),
            pl.BlockSpec((hid, D), lambda e: (e, 0)),
            full_spec((ROWS8, D)),
        ],
        out_shape=[
            jax.ShapeDtypeStruct((length, D), bf16),
            jax.ShapeDtypeStruct((length, D), f32),
            jax.ShapeDtypeStruct((D, wide), f32),
            jax.ShapeDtypeStruct((D, wide), f32),
            jax.ShapeDtypeStruct((wide, D), f32),
            jax.ShapeDtypeStruct((ROWS8, D), f32),
        ],
        scratch_shapes=[
            pltpu.VMEM((length, D), bf16),
            pltpu.VMEM((length, D), f32),
            pltpu.VMEM((ROWS8, length), f32),
            pltpu.VMEM((ROWS8, length), f32),
        ],
        compiler_params=pltpu.CompilerParams(vmem_limit_bytes=60 << 20),
        name="moe",
    )(h1, g2, wr_t, slot_row, slot_col, dy, w_gate, w_up, w_down, other, other, other)


def swap_tensor(values):
    size = lax.axis_size("tensor")
    return lax.ppermute(values, "tensor", [(i, i ^ 1) for i in range(size)])


def gather_other(w_gate, w_up, w_down, w_out):
    parts = lax.axis_size("dp")
    packed = jnp.concatenate(
        [
            jnp.concatenate([w_gate[e] for e in range(EXPERTS)], axis=1),
            jnp.concatenate([w_up[e] for e in range(EXPERTS)], axis=1),
            w_down.reshape(-1, D),
            w_out,
        ],
        axis=0,
    )
    rows = packed.shape[0] // parts
    share = lax.dynamic_slice_in_dim(packed, lax.axis_index("dp") * rows, rows, 0).astype(f32)
    return lax.all_gather(swap_tensor(share), "dp", axis=0, tiled=True)


def sum_dp(values):
    share = lax.psum_scatter(values, "dp", scatter_dimension=0, tiled=True)
    return lax.all_gather(share, "dp", axis=0, tiled=True)


def per_device(
    layer_input,
    segments,
    expert_choice,
    dispatch_order,
    norm_gain_one,
    w_query,
    w_key,
    w_value,
    w_out,
    norm_gain_two,
    w_router,
    w_gate,
    w_up,
    w_down,
    out_grad,
):
    length = layer_input.shape[0]
    q_cols = w_query.shape[1]
    kv_cols = w_key.shape[1]
    hid = w_down.shape[1]
    wide = EXPERTS * hid
    other = gather_other(w_gate, w_up, w_down, w_out)
    slot_row = route(expert_choice.T, dispatch_order)
    slot_col = slot_row.T
    seg_row = segments
    seg_col = segments.reshape(length, 1)

    residual = layer_input.astype(f32)
    inverse_one = lax.rsqrt(jnp.mean(residual * residual, axis=-1, keepdims=True) + norm_eps)
    normed_one = residual * inverse_one
    input_one = (normed_one * norm_gain_one).astype(bf16)
    w_qkv = jnp.concatenate([w_query, w_key, w_value], axis=1)
    qkv = jnp.dot(input_one, w_qkv, preferred_element_type=f32).astype(bf16)
    attended = attn_fwd(qkv, seg_col, seg_row, q_cols)
    attended_other = swap_tensor(attended)

    wr_t = jnp.pad(w_router.T.astype(f32), ((0, ROWS8 - EXPERTS), (0, 0)))
    out_at = (2 * D + wide) // q_cols
    middle = out_project(layer_input, attended, attended_other, w_out, other, out_at)
    block_out, grad_middle, grad_gate, grad_up, grad_down, small = moe(
        middle,
        other,
        norm_gain_two[None, :],
        wr_t,
        slot_row,
        slot_col,
        out_grad,
        w_gate,
        w_up,
        w_down,
    )
    expert_sum = sum_dp(jnp.concatenate([grad_gate, grad_up, grad_down], axis=0))

    grad_attn = grad_middle.astype(bf16)
    attended_low = attended.astype(bf16)
    grad_wout = jnp.einsum("tn,td->nd", attended_low, grad_attn, preferred_element_type=f32)
    grad_heads = jnp.einsum("td,nd->tn", grad_attn, w_out, preferred_element_type=f32).astype(bf16)
    dq, dk, dv = attn_bwd(qkv, grad_heads, seg_col, seg_row, q_cols)
    dqkv = jnp.concatenate([dq, dk, dv], axis=1)
    grad_wqkv = jnp.einsum("td,tn->dn", input_one, dqkv, preferred_element_type=f32)
    part = jnp.einsum("tn,dn->td", dqkv, w_qkv, preferred_element_type=f32)
    grad_input_one = part + swap_tensor(part)
    scaled = grad_input_one * norm_gain_one
    mean_term = jnp.mean(scaled * normed_one, axis=-1, keepdims=True)
    grad_gain_one = jnp.sum(grad_input_one * normed_one, axis=0)
    grad_input = grad_middle + inverse_one * (scaled - normed_one * mean_term)

    small = jnp.concatenate([small[: EXPERTS + 1], grad_gain_one[None, :]], axis=0)
    packed = jnp.concatenate([grad_wqkv, grad_wout, small], axis=0)
    parts = lax.axis_size("dp")
    packed = jnp.pad(packed, ((0, -packed.shape[0] % (8 * parts)), (0, 0)))
    attn_sum = sum_dp(packed)

    sum_gate = jnp.stack([expert_sum[:D, hid * e : hid * (e + 1)] for e in range(EXPERTS)])
    sum_up = jnp.stack([expert_sum[D : 2 * D, hid * e : hid * (e + 1)] for e in range(EXPERTS)])
    sum_down = expert_sum[2 * D : 2 * D + wide].reshape(w_down.shape)
    at = D + q_cols
    return (
        block_out,
        grad_input,
        attn_sum[at + EXPERTS + 1],
        attn_sum[:D, :q_cols],
        attn_sum[:D, q_cols : q_cols + kv_cols],
        attn_sum[:D, q_cols + kv_cols :],
        attn_sum[D:at],
        attn_sum[at + EXPERTS],
        attn_sum[at : at + EXPERTS].T,
        sum_gate,
        sum_up,
        sum_down,
    )


def solution(mesh):
    in_specs = (
        P("dp", None),
        P("dp", None),
        P("dp", None),
        P("dp", None),
        P(),
        P(None, "tensor"),
        P(None, "tensor"),
        P(None, "tensor"),
        P("tensor", None),
        P(),
        P(),
        P(None, None, "tensor"),
        P(None, None, "tensor"),
        P(None, "tensor", None),
        P("dp", None),
    )
    out_specs = (
        P("dp", None),
        P("dp", None),
        P(),
        P(None, "tensor"),
        P(None, "tensor"),
        P(None, "tensor"),
        P("tensor", None),
        P(),
        P(),
        P(None, None, "tensor"),
        P(None, None, "tensor"),
        P(None, "tensor", None),
    )
    return jax.shard_map(
        per_device, mesh=mesh, in_specs=in_specs, out_specs=out_specs, check_vma=False
    )
```

time: 2480 us -> 791 us (0.32)
  local copies, waits for them, and re-layouts: 1310 us -> 54.6 us
  other arithmetic: 321 us -> 26.5 us
  waiting for transfers between devices: 703 us -> 552 us
  Pallas kernels: 0 us -> 115 us
  matrix products: 122 us -> 16.9 us
    slice x19 -> x5, local copies, waits for them, and re-layouts: 1130 us -> 15.6 us  [the longest x1 4.79 us: per_device(): sum_down = expert_sum[2 * D:2 * D + wide].reshape(w_down.shape)]
    unnamed x6 -> x5, waiting for transfers between devices: 331 us -> 0.08 us
    psum x3 -> x0, waiting for transfers between devices: 282 us -> none  [the longest x1 177 us: per_device(): routed_total = lax.psum(routed_part, 'tensor')]
    reduce_scatter x0 -> x2, waiting for transfers between devices: none -> 216 us  [sum_dp(): share = lax.psum_scatter(values, 'dp', scatter_dimension=0, tiled=True)]
    all_gather x1 -> x0, other arithmetic: 201 us -> none  [per_device(): lax.all_gather(joined_shares, 'dp', axis=0, tiled=True)]
    ppermute x0 -> x3, waiting for transfers between devices: none -> 143 us  [swap_tensor(): return lax.ppermute(values, 'tensor', [(i, i ^ 1) for i in range(size)])]
    pallas_call x0 -> x5, Pallas kernels: none -> 115 us  [the longest x1 65.7 us: moe(): pl.pallas_call(moe_kernel, grid=(EXPERTS,), in_specs=[full_spec((length,...]
    dot_general x36 -> x5, matrix products: 122 us -> 16.9 us  [the longest x1 4.62 us: per_device(): jnp.einsum('td,tn->dn', input_one, dqkv, preferred_element_type=f32)]
  transfers between devices with their start and end apart: 5 -> 8, of which waited for: 5 -> 8; matrix products, arithmetic and copies ran while one was open for 6% -> 6% of each run, Pallas kernels for 0% -> 3%
where the time goes in v2:
time: 791 us; the launch traced here: 786 us
  waiting for transfers between devices  552 us (70%)
  Pallas kernels  115 us (15%)
  local copies, waits for them, and re-layouts  54.6 us (7%)
  other arithmetic  26.5 us (3%)
  matrix products  16.9 us (2%)
  between operations  14.3 us (2%)
    reduce_scatter x2, waiting for transfers between devices, sum_dp(): share = lax.psum_scatter(values, 'dp', scatter_dimension=0, tiled=True)  216 us
    all_gather x2, waiting for transfers between devices, sum_dp(): return lax.all_gather(share, 'dp', axis=0, tiled=True)  149 us
    ppermute x3, waiting for transfers between devices, swap_tensor(): return lax.ppermute(values, 'tensor', [(i, i ^ 1) for i in range(size)])  143 us
    pallas_call x1, Pallas kernels, moe(): pl.pallas_call(moe_kernel, grid=(EXPERTS,), in_specs=[full_spec((length,...  65.7 us
    all_gather x1, waiting for transfers between devices, gather_other(): return lax.all_gather(swap_tensor(share), 'dp', axis=0, tiled=True)  43.5 us
    pallas_call x1, Pallas kernels, attn_bwd(): pl.pallas_call(functools.partial(attn_bwd_kernel, 256), grid=(pairs,), in...  21 us
    concatenate x1, local copies, waits for them, and re-layouts, per_device(): packed = jnp.concatenate([grad_wqkv, grad_wout, small], axis=0)  16.4 us
    pallas_call x1, Pallas kernels, attn_fwd(): pl.pallas_call(functools.partial(attn_fwd_kernel, 256), grid=(pairs,), in...  16.1 us
  transfers between devices with their start and end apart: 8, of which 8 were waited for; matrix products, arithmetic and copies ran while one was open for 6% of the time, Pallas kernels for 3%

profile of v2, /device:TPU:0, one launch (start us, length us, event | category | flops | bytes accessed | tf_op | source)
XLA Modules:
  0.0 785.6 jit_solution(2745142188712644115)
XLA Ops:
  7.3 2.6 slice_bitcast_fusion.11
  9.8 0.3 copy-done.11
  10.1 0.3 copy-done.12
  10.3 2.7 fusion.26
  13.1 3.0 collective-permute-start.1
  16.1 20.3 %collective-permute-done.1 = f32[224,1024]{1,0:T(8,128)S(1)} collective-permute-done((f32[224,1024]{1,0:T(8,128)S(1)}, f32[224,1024]{1,0:T(8,128)S(1)}, u32[]{:S(2)}, u32[]{:S(2)}) %collective-permute-start.1) | collective-permute-done | bytes 917536 | tf_op jit(solution)/shard_map/ppermute | solution.py:422
  36.5 0.9 copy-done.14
  37.7 1.3 constant_dynamic-update-slice_fusion.2
  39.1 1.1 constant_dynamic-update-slice_fusion.1
  40.2 1.1 constant_dynamic-update-slice_fusion
  41.3 0.5 fusion.10
  41.8 0.8 copy-done.15
  42.6 3.7 convolution_convert_fusion.q_ref.k_ref.v_ref
  46.3 16.1 %attn_fwd.1.oa_ref = f32[1024,512]{1,0:T(8,128)S(1)} custom-call(bf16[1024,1024]{1,0:T(8,128)(2,1)} %convolution_convert_fusion.q_ref.k_ref.v_ref, bf16[1024,1024]{1,0:T(8,128)(2,1)} %convolution_convert_fusion.q_ref.k_ref.v_ref, bf16[1024,1024]{1,0:T(8,128)(2,1)} %convolution_convert_fusion.q_ref.k_ref.v_ref, s32[1024,1]{1,0:T(8,128)S(1)} %copy.28.segc_ref, ...), custom_call_target="tpu_custom_call" | custom-call | tf_op jit(solution)/shard_map/attn_fwd/pallas_call | solution.py:125
  62.4 1.8 collective-permute-start
  64.3 4.7 route.1.slotr_ref
  68.9 1.0 copy.29
  69.9 0.6 pad_convert_fusion.wr_ref
  70.6 38.8 %collective-permute-done.ob_ref = f32[1024,512]{1,0:T(8,128)} collective-permute-done((f32[1024,512]{1,0:T(8,128)S(1)}, f32[1024,512]{1,0:T(8,128)}, u32[]{:S(2)}, u32[]{:S(2)}) %collective-permute-start) | collective-permute-done | bytes 2097184 | tf_op jit(solution)/shard_map/ppermute | solution.py:422
  109.4 43.5 %all-gather.4.cloned.1.call-done.wox_ref.wgx_ref.wux_ref.wdx_ref = f32[3584,1024]{1,0:T(8,128)} async-done(((f32[224,1024]{1,0:T(8,128)}), f32[3584,1024]{1,0:T(8,128)}) %all-gather.4.cloned.1.call-update) | async-done | bytes 14680080 | tf_op jit(solution)/shard_map/all_gather | solution.py:438
  152.9 7.7 out_project.1.h_s
  160.6 65.7 %moe.1 = (bf16[1024,1024]{1,0:T(8,128)(2,1)}, f32[1024,1024]{1,0:T(8,128)}, f32[1024,1024]{1,0:T(8,128)}, f32[1024,1024]{1,0:T(8,128)}, f32[1024,1024]{1,0:T(8,128)}, /*index=5*/f32[8,1024]{1,0:T(8,128)}) custom-call(f32[1024,1024]{1,0:T(8,128)} %out_project.1.h_s, f32[1,1024]{1,0:T(1,128)} %bitcast.58, f32[8,1024]{1,0:T(8,128)} %pad_convert_fusion.wr_ref, ...), custom_call_target="tpu_custom_call" | custom-call | tf_op jit(solution)/shard_map/moe/pallas_call | solution.py:376
  226.4 3.5 convolution_convert_fusion.1.do_ref
  229.9 21.0 %attn_bwd.1 = (bf16[1024,512]{1,0:T(8,128)(2,1)S(1)}, bf16[1024,256]{1,0:T(8,128)(2,1)S(1)}, bf16[1024,256]{1,0:T(8,128)(2,1)S(1)}) custom-call(bf16[1024,1024]{1,0:T(8,128)(2,1)} %convolution_convert_fusion.q_ref.k_ref.v_ref, bf16[1024,1024]{1,0:T(8,128)(2,1)} %convolution_convert_fusion.q_ref.k_ref.v_ref, ...), custom_call_target="tpu_custom_call" | custom-call | tf_op jit(solution)/shard_map/attn_bwd/pallas_call | solution.py:196
  251.2 2.4 fusion.29
  253.7 1.5 collective-permute-start.2
  255.2 2.6 fusion.11
  257.8 4.6 fusion.15
  262.5 84.0 %collective-permute-done.2 = f32[1024,1024]{1,0:T(8,128)S(1)} collective-permute-done((f32[1024,1024]{1,0:T(8,128)S(1)}, f32[1024,1024]{1,0:T(8,128)S(1)}, u32[]{:S(2)}, u32[]{:S(2)}) %collective-permute-start.2) | collective-permute-done | bytes 4194336 | tf_op jit(solution)/shard_map/ppermute | solution.py:422
  346.5 1.5 fusion.9
  348.0 0.6 copy-done.9
  348.6 16.4 %concatenate.26 = f32[1542,1024]{1,0:T(8,128)} concatenate(f32[1024,1024]{1,0:T(8,128)} %fusion.15, f32[512,1024]{1,0:T(8,128)} %fusion.11, f32[5,1024]{1,0:T(8,128)S(1)} %bitcast.55, f32[1,1024]{1,0:T(1,128)S(1)} %bitcast.56), dimensions={0} | concatenate | bytes 12632064 | tf_op jit(solution)/shard_map/concatenate | solution.py:515
  365.0 6.7 pad.12
  371.7 9.7 %pad_maximum_fusion = f32[3072,1024]{1,0:T(8,128)} fusion(f32[1024,1024]{1,0:T(8,128)} %get-tuple-element.29, f32[1024,1024]{1,0:T(8,128)} %get-tuple-element.28, f32[1024,1024]{1,0:T(8,128)} %get-tuple-element.27), kind=kLoop, calls=%fused_computation | loop fusion | flops 6291456 | bytes 25165824 | tf_op jit(solution)/shard_map/concatenate | solution.py:498
  381.5 76.9 %reduce-scatter.3.cloned.1.call-done = f32[104,1024]{1,0:T(8,128)} async-done(((f32[1664,1024]{1,0:T(8,128)}), f32[104,1024]{1,0:T(8,128)}) %reduce-scatter.3.cloned.1.call-update) | async-done | bytes 426000 | tf_op jit(solution)/shard_map/reduce_scatter | solution.py:442
  458.5 138.8 %reduce-scatter.5.cloned.1.call-done = f32[192,1024]{1,0:T(8,128)} async-done(((f32[3072,1024]{1,0:T(8,128)}), f32[192,1024]{1,0:T(8,128)}) %reduce-scatter.5.cloned.1.call-update) | async-done | bytes 786448 | tf_op jit(solution)/shard_map/reduce_scatter | solution.py:442
  597.3 7.0 fusion.8
  604.2 59.6 %all-gather.6.cloned.1.call-done = f32[1664,1024]{1,0:T(8,128)} async-done(((f32[104,1024]{1,0:T(8,128)}), f32[1664,1024]{1,0:T(8,128)}) %all-gather.6.cloned.1.call-update) | async-done | bytes 6815760 | tf_op jit(solution)/shard_map/all_gather | solution.py:443
  663.8 3.2 slice.104
  667.0 3.1 slice.101
  670.0 1.4 fusion.27
  671.5 1.4 slice_bitcast_fusion.16
  672.8 3.1 fusion.28
  675.9 89.5 %all-gather.8.cloned.1.call-done = f32[3072,1024]{1,0:T(8,128)} async-done(((f32[192,1024]{1,0:T(8,128)}), f32[3072,1024]{1,0:T(8,128)}) %all-gather.8.cloned.1.call-update) | async-done | bytes 12582928 | tf_op jit(solution)/shard_map/all_gather | solution.py:443
  765.5 4.0 slice_bitcast_fusion.3
  769.5 2.3 pad_maximum_fusion.2
  771.8 2.3 pad_maximum_fusion.1
  774.1 4.8 slice.115
  (51 shorter events, 0.9 us)
Async XLA Ops:
  7.2 145.7 %all-gather.4.cloned.1.call-start = ((), (), s32[]{:S(2)}) async-start(), calls=%async_computation.2 | async-start | bytes 15597568 | tf_op jit(solution)/shard_map/all_gather | solution.py:438
  7.2 2.9 copy-start.11
  7.2 3.1 copy-start.12
  10.3 27.1 %copy-start.3 = (s32[1,1024]{1,0:T(1,128)S(1)}, s32[1,1024]{1,0:T(1,128)}, u32[]{:S(2)}) copy-start(s32[1,1024]{1,0:T(1,128)} %segr_ref.3) | copy-start | bytes 12292
  13.1 28.2 %copy-start.6 = (bf16[1024,1024]{1,0:T(8,128)(2,1)S(1)}, bf16[1024,1024]{1,0:T(8,128)(2,1)}, u32[]{:S(2)}) copy-start(bf16[1024,1024]{1,0:T(8,128)(2,1)} %x_ref.1) | copy-start | bytes 6291460
  13.1 29.6 %copy-start.18 = (f32[1024]{0:T(1024)S(1)}, f32[1024]{0:T(1024)}, u32[]{:S(2)}) copy-start(f32[1024]{0:T(1024)} %param.19) | copy-start | bytes 12292
  13.1 23.4 %collective-permute-start.1 = (f32[224,1024]{1,0:T(8,128)S(1)}, f32[224,1024]{1,0:T(8,128)S(1)}, u32[]{:S(2)}, u32[]{:S(2)}) collective-permute-start(f32[224,1024]{1,0:T(8,128)S(1)} %fusion.26), channel_id=1, source_target_pairs={{0,1},{1,0},{2,3},{3,2},{4,5},{5,4},{6,7},{7,6},{8,9},{9,8},{10,11... | collective-permute-start | bytes 2752520 | tf_op jit(solution)/shard_map/ppermute | solution.py:422
  36.5 0.9 copy-start.14
  37.4 421.0 %reduce-scatter.3.cloned.1.call-start = ((), (), s32[]{:S(2)}) async-start(), calls=%async_computation.3 | async-start | bytes 7241728 | tf_op jit(solution)/shard_map/reduce_scatter | solution.py:442
  41.3 1.3 copy-start.15
  46.3 17.9 %copy-start.4 = (s32[1024,2]{0,1:T(2,128)S(1)}, s32[1024,2]{0,1:T(2,128)}, u32[]{:S(2)}) copy-start(s32[1024,2]{0,1:T(2,128)} %param.17) | copy-start | bytes 24580
  46.3 17.9 %copy-start.5 = (s32[1,2048]{1,0:T(1,128)S(1)}, s32[1,2048]{1,0:T(1,128)}, u32[]{:S(2)}) copy-start(s32[1,2048]{1,0:T(1,128)} %order_ref.1) | copy-start | bytes 24580
  46.3 23.6 %copy-start.19 = (bf16[1024,4]{0,1:T(4,128)(2,1)S(1)}, bf16[1024,4]{0,1:T(4,128)(2,1)}, u32[]{:S(2)}) copy-start(bf16[1024,4]{0,1:T(4,128)(2,1)} %param.25) | copy-start | bytes 24580
  62.4 90.5 %copy-start = (f32[1024,512]{1,0:T(8,128)}, f32[1024,512]{1,0:T(8,128)S(1)}, u32[]{:S(2)}) copy-start(f32[1024,512]{1,0:T(8,128)S(1)} %attn_fwd.1.oa_ref) | copy-start | bytes 6291460
  62.4 46.9 %collective-permute-start = (f32[1024,512]{1,0:T(8,128)S(1)}, f32[1024,512]{1,0:T(8,128)}, u32[]{:S(2)}, u32[]{:S(2)}) collective-permute-start(f32[1024,512]{1,0:T(8,128)S(1)} %attn_fwd.1.oa_ref), channel_id=1, source_target_pairs={{0,1},{1,0},{2,3},{3,2},{4,5},{5,4},{6,7},{7,6},{8,9},{9,8},{10,11... | collective-permute-start | bytes 6291464 | tf_op jit(solution)/shard_map/ppermute | solution.py:422
  68.9 91.7 %copy-start.2 = (s32[8,1024]{1,0:T(8,128)}, s32[8,1024]{1,0:T(8,128)S(1)}, u32[]{:S(2)}) copy-start(s32[8,1024]{1,0:T(8,128)S(1)} %route.1.slotr_ref) | copy-start | bytes 98308
  160.6 65.7 %copy-start.13 = (bf16[512,1024]{1,0:T(8,128)(2,1)S(1)}, bf16[512,1024]{1,0:T(8,128)(2,1)}, u32[]{:S(2)}) copy-start(bf16[512,1024]{1,0:T(8,128)(2,1)} %wo_ref.1) | copy-start | bytes 3145732
  229.9 21.3 %copy-start.16 = (bf16[1024,1024]{1,0:T(8,128)(2,1)S(1)}, bf16[1024,1024]{1,0:T(8,128)(2,1)}, u32[]{:S(2)}) copy-start(bf16[1024,1024]{1,0:T(8,128)(2,1)} %copy-done.15) | copy-start | bytes 6291460
  251.2 4.0 copy-start.1
  251.2 4.0 copy-start.10
  253.7 92.8 %copy-start.8 = (f32[1024,1024]{1,0:T(8,128)}, f32[1024,1024]{1,0:T(8,128)S(1)}, u32[]{:S(2)}) copy-start(f32[1024,1024]{1,0:T(8,128)S(1)} %fusion.29) | copy-start | bytes 12582916
  253.7 4.2 copy-start.7
  253.7 92.8 %collective-permute-start.2 = (f32[1024,1024]{1,0:T(8,128)S(1)}, f32[1024,1024]{1,0:T(8,128)S(1)}, u32[]{:S(2)}, u32[]{:S(2)}) collective-permute-start(f32[1024,1024]{1,0:T(8,128)S(1)} %fusion.29), channel_id=1, source_target_pairs={{0,1},{1,0},{2,3},{3,2},{4,5},{5,4},{6,7},{7,6},{8,9},{9,8},{10,11... | collective-permute-start | bytes 12582920 | tf_op jit(solution)/shard_map/ppermute | solution.py:422
  262.5 86.1 %copy-start.17 = (f32[8,1024]{1,0:T(8,128)S(1)}, f32[8,1024]{1,0:T(8,128)}, u32[]{:S(2)}) copy-start(f32[8,1024]{1,0:T(8,128)} %get-tuple-element.26) | copy-start | bytes 98308
  346.5 2.1 copy-start.9
  371.7 225.6 %reduce-scatter.5.cloned.1.call-start = ((), (), s32[]{:S(2)}) async-start(), calls=%async_computation.5 | async-start | bytes 13369344 | tf_op jit(solution)/shard_map/reduce_scatter | solution.py:442
  381.5 282.3 %all-gather.6.cloned.1.call-start = ((), (), s32[]{:S(2)}) async-start(), calls=%async_computation.4 | async-start | bytes 7241728 | tf_op jit(solution)/shard_map/all_gather | solution.py:443
  458.4 307.1 %all-gather.8.cloned.1.call-start = ((), (), s32[]{:S(2)}) async-start(), calls=%async_computation.6 | async-start | bytes 13369344 | tf_op jit(solution)/shard_map/all_gather | solution.py:443
Sparse Core Ops, SparseCore 0:
  37.5 115.3 all-gather.3
  371.8 86.5 reduce-scatter.2
  463.0 134.1 reduce-scatter.4
  599.6 64.1 all-gather.5
  666.2 99.2 all-gather.7
